TPU v7x, 32 devices: a whole 2x2x4 slice. The times are simulated.
32 devices in a mesh: pipe: 4 (over x, core), dp: 2 (over y), tensor: 4 (over z).
Axes of the slice: x: 2, y: 2, z: 4, core: 2. Of those that a mesh axis runs over, the one named last changes fastest.
Arguments:
- grad_top: bfloat16 [2, 128, 12288], P(None, None, ('dp', 'tensor')), may hold values from -1.1953125 to 1.1953125
- inputs: bfloat16 [4, 2, 128, 12288], P('pipe', None, None, ('dp', 'tensor')), may hold values from -6 to 6
- pre: bfloat16 [4, 2, 128, 6144], P('pipe', None, 'dp', 'tensor'), may hold values from -6 to 6
- weight_in: bfloat16 [4, 6144, 12288], P('pipe', 'tensor', 'dp'), may hold values from -0.0546875 to 0.0546875
- weight_out: bfloat16 [4, 6144, 12288], P('pipe', 'tensor', 'dp'), may hold values from -0.0546875 to 0.0546875
Outputs:
- weight_in_grad: bfloat16 [4, 6144, 12288], P('pipe', 'tensor', 'dp')
- weight_out_grad: bfloat16 [4, 6144, 12288], P('pipe', 'tensor', 'dp')
- section_grads: bfloat16 [4, 2, 128, 12288], P('pipe', None, None, ('dp', 'tensor'))
All inputs are finite; a program needn't handle non-finite values.
Results may differ from a plain program's by a relative error of at most 0.024.
Values may be sent and summed in bfloat16 or wider, within the bound.
A program may use at most 512 MiB of HBM per device.

v0:
```python
import math
import jax
import jax.numpy as jnp
from jax import lax
from jax.sharding import PartitionSpec as P


def shifted(block, axis, distance):
    devices = range(lax.axis_size(axis))
    route = [(i - distance, i) for i in devices if i - distance in devices]
    return lax.ppermute(block, axis, route)


def gelu_pair(values):
    root_coef = math.sqrt(2.0 / math.pi)
    inner = root_coef * (values + 0.044715 * values * values * values)
    tangent = jnp.tanh(inner)
    activ = 0.5 * values * (1.0 + tangent)
    slope = 0.5 * (1.0 + tangent) + 0.5 * values * (1.0 - tangent * tangent) * root_coef * (
        1.0 + 3.0 * 0.044715 * values * values
    )
    return (activ, slope)


def on_device(grad_top, inputs, pre, weight_in, weight_out):
    sections = lax.axis_size("pipe")
    section = lax.axis_index("pipe")
    micro = grad_top.shape[0]
    local_in = weight_in[0]
    local_out = weight_out[0]
    contract = (((0,), (0,)), ((), ()))
    accum_in = jnp.zeros(local_in.shape, jnp.float32)
    accum_out = jnp.zeros(local_out.shape, jnp.float32)
    grads_out = jnp.zeros(grad_top.shape, jnp.bfloat16)
    outgoing = grad_top[0]
    for timestep in range(micro + sections - 1):
        micro_index = timestep - (sections - 1 - section)
        valid = jnp.logical_and(micro_index >= 0, micro_index < micro)
        clipped = jnp.clip(micro_index, 0, micro - 1)
        top_grad = lax.dynamic_index_in_dim(grad_top, clipped, 0, False)
        if timestep == 0:
            current = top_grad
        else:
            received = shifted(outgoing, "pipe", -1)
            current = jnp.where(section == sections - 1, top_grad, received)
        layer_input = lax.dynamic_index_in_dim(inputs[0], clipped, 0, False)
        pre_local = lax.dynamic_index_in_dim(pre[0], clipped, 0, False)
        grad_cols, input_cols = (
            lax.all_gather(current, "tensor", axis=1, tiled=True),
            lax.all_gather(layer_input, "tensor", axis=1, tiled=True),
        )
        head_part = lax.dot_general(
            grad_cols, local_out, (((1,), (1,)), ((), ())), preferred_element_type=jnp.float32
        )
        head_grad = lax.psum(head_part.astype(jnp.bfloat16), "dp").astype(jnp.float32)
        pre_all = lax.all_gather(pre_local, "dp", axis=0, tiled=True)
        activ, slope = gelu_pair(pre_all.astype(jnp.float32))
        head_delta = (head_grad * slope).astype(jnp.bfloat16)
        activated = activ.astype(jnp.bfloat16)
        partial_value = jnp.dot(head_delta, local_in, preferred_element_type=jnp.float32)
        summed = lax.psum_scatter(
            partial_value.astype(jnp.bfloat16), "tensor", scatter_dimension=1, tiled=True
        ).astype(jnp.float32)
        new_grad = (current.astype(jnp.float32) + summed).astype(jnp.bfloat16)
        out_term = lax.dot_general(
            activated, grad_cols, contract, preferred_element_type=jnp.float32
        )
        in_term = lax.dot_general(
            head_delta, input_cols, contract, preferred_element_type=jnp.float32
        )
        accum_out = accum_out + jnp.where(valid, out_term, 0.0)
        accum_in = accum_in + jnp.where(valid, in_term, 0.0)
        previous = lax.dynamic_index_in_dim(grads_out, clipped, 0, False)
        grads_out = lax.dynamic_update_index_in_dim(
            grads_out, jnp.where(valid, new_grad, previous), clipped, 0
        )
        outgoing = new_grad
    return (
        accum_in.astype(jnp.bfloat16)[None],
        accum_out.astype(jnp.bfloat16)[None],
        grads_out[None],
    )


def solution(mesh):
    placed = (
        P(None, None, ("dp", "tensor")),
        P("pipe", None, None, ("dp", "tensor")),
        P("pipe", None, "dp", "tensor"),
        P("pipe", "tensor", "dp"),
        P("pipe", "tensor", "dp"),
    )
    return jax.shard_map(
        on_device,
        mesh=mesh,
        in_specs=placed,
        out_specs=(
            P("pipe", "tensor", "dp"),
            P("pipe", "tensor", "dp"),
            P("pipe", None, None, ("dp", "tensor")),
        ),
        check_vma=False,
    )
```

profile of v0, /device:TPU:0, one launch (start us, length us, event | category | flops | bytes accessed | tf_op | source)
XLA Modules:
  0.0 836.4 jit_solution(14600435980791823250)
XLA Ops:
  7.2 1.8 constant_dynamic-slice_fusion.13
  9.1 40.8 %all-gather.30.cloned.1.call-done = bf16[1,128,6144]{2,1,0:T(8,128)(2,1)} async-done(((bf16[1,128,1536]{2,1,0:T(8,128)(2,1)}), bf16[1,128,6144]{2,1,0:T(8,128)(2,1)}) %all-gather.30.cloned.1.call-update) | async-done | bytes 1572880 | tf_op jit(solution)/shard_map/all_gather | solution.py:49
  49.9 14.0 %fusion.37 = bf16[128,1536]{1,0:T(8,128)(2,1)} fusion(bf16[1,1536,6144]{2,1,0:T(8,128)(2,1)} %param.9, bf16[1,128,6144]{2,1,0:T(8,128)(2,1)} %all-gather.30.cloned.1.call-done), kind=kOutput, calls=%fused_computation.29 | convolution fusion | flops 2416115712 | bytes 20840448 | tf_op jit(solution)/shard_map/dot_general | solution.py:52
  64.0 0.8 constant_dynamic-slice_fusion.4
  64.8 9.4 %all-gather.1 = bf16[1,1,128,1536]{3,2,1,0:T(8,128)(2,1)S(1)} all-gather(bf16[1,1,64,1536]{3,2,1,0:T(8,128)(2,1)S(1)} %get-tuple-element.19), channel_id=3, replica_groups=mesh['pipe'=4,'dp'=2,'tensor'=4] {'dp'}, dimensions={2}, use_global_device_ids=true | all-gather | bytes 589824 | tf_op jit(solution)/shard_map/all_gather | solution.py:56
  74.2 15.2 %all-reduce.6.cloned.1.call-done = bf16[128,1536]{1,0:T(8,128)(2,1)} async-done(((bf16[128,1536]{1,0:T(8,128)(2,1)}), bf16[128,1536]{1,0:T(8,128)(2,1)}) %all-reduce.6.cloned.1.call-update) | async-done | bytes 393232 | tf_op jit(solution)/shard_map/psum | solution.py:55
  89.5 10.7 %fusion.22 = bf16[128,6144]{1,0:T(8,128)(2,1)} fusion(bf16[1,1536,6144]{2,1,0:T(8,128)(2,1)} %param.8, bf16[128,1536]{1,0:T(8,128)(2,1)} %all-reduce.6.cloned.1.call-done, bf16[1,1,128,1536]{3,2,1,0:T(8,128)(2,1)S(1)} %all-gather.1), kind=kOutput, calls=%fused_computation.24 | convolution fusion | flops 2420834304 | bytes 21233664 | tf_op jit(solution)/shard_map/dot_general | solution.py:60
  100.2 35.5 %reduce-scatter.6.cloned.1.call-done = bf16[128,1536]{1,0:T(8,128)(2,1)} async-done(((bf16[128,6144]{1,0:T(8,128)(2,1)}), bf16[128,1536]{1,0:T(8,128)(2,1)}) %reduce-scatter.6.cloned.1.call-update) | async-done | bytes 393232 | tf_op jit(solution)/shard_map/reduce_scatter | solution.py:61
  135.8 1.1 bitcast_dynamic-update-slice_fusion.3
  137.0 1.3 collective-permute-start
  138.3 2.3 collective-permute-done
  140.6 0.8 bitcast_select_fusion.6
  141.7 39.8 %all-gather.22.cloned.1.call-done = bf16[128,6144]{1,0:T(8,128)(2,1)} async-done(((bf16[128,1536]{1,0:T(8,128)(2,1)}), bf16[128,6144]{1,0:T(8,128)(2,1)}) %all-gather.22.cloned.1.call-update) | async-done | bytes 1572880 | tf_op jit(solution)/shard_map/all_gather | solution.py:49
  181.5 14.0 %fusion.40 = bf16[128,1536]{1,0:T(8,128)(2,1)} fusion(bf16[128,6144]{1,0:T(8,128)(2,1)} %all-gather.22.cloned.1.call-done, bf16[1,1536,6144]{2,1,0:T(8,128)(2,1)} %param.9), kind=kOutput, calls=%fused_computation.30 | convolution fusion | flops 2416115712 | bytes 20840448 | tf_op jit(solution)/shard_map/dot_general | solution.py:52
  195.6 8.2 all-gather.3
  203.8 16.6 %all-reduce.8.cloned.1.call-done = bf16[128,1536]{1,0:T(8,128)(2,1)} async-done(((bf16[128,1536]{1,0:T(8,128)(2,1)}), bf16[128,1536]{1,0:T(8,128)(2,1)}) %all-reduce.8.cloned.1.call-update) | async-done | bytes 393232 | tf_op jit(solution)/shard_map/psum | solution.py:55
  220.4 10.7 %fusion.25 = bf16[128,6144]{1,0:T(8,128)(2,1)} fusion(bf16[1,1536,6144]{2,1,0:T(8,128)(2,1)} %param.8, bf16[128,1536]{1,0:T(8,128)(2,1)} %all-reduce.8.cloned.1.call-done, bf16[1,1,128,1536]{3,2,1,0:T(8,128)(2,1)S(1)} %all-gather.3), kind=kOutput, calls=%fused_computation.25 | convolution fusion | flops 2420834304 | bytes 21233664 | tf_op jit(solution)/shard_map/dot_general | solution.py:60
  231.2 35.5 %reduce-scatter.8.cloned.1.call-done = bf16[128,1536]{1,0:T(8,128)(2,1)} async-done(((bf16[128,6144]{1,0:T(8,128)(2,1)}), bf16[128,1536]{1,0:T(8,128)(2,1)}) %reduce-scatter.8.cloned.1.call-update) | async-done | bytes 393232 | tf_op jit(solution)/shard_map/reduce_scatter | solution.py:61
  266.7 1.2 bitcast_dynamic-update-slice_fusion.2
  267.9 1.3 collective-permute-start.1
  269.2 2.3 collective-permute-done.1
  272.9 39.5 %all-gather.24.cloned.1.call-done = bf16[128,6144]{1,0:T(8,128)(2,1)} async-done(((bf16[128,1536]{1,0:T(8,128)(2,1)}), bf16[128,6144]{1,0:T(8,128)(2,1)}) %all-gather.24.cloned.1.call-update) | async-done | bytes 1572880 | tf_op jit(solution)/shard_map/all_gather | solution.py:49
  312.4 14.0 %fusion.43 = bf16[128,1536]{1,0:T(8,128)(2,1)} fusion(bf16[128,6144]{1,0:T(8,128)(2,1)} %all-gather.24.cloned.1.call-done, bf16[1,1536,6144]{2,1,0:T(8,128)(2,1)} %param.9), kind=kOutput, calls=%fused_computation.31 | convolution fusion | flops 2416115712 | bytes 20840448 | tf_op jit(solution)/shard_map/dot_general | solution.py:52
  326.5 8.3 all-gather.5
  334.7 16.6 %all-reduce.10.cloned.1.call-done = bf16[128,1536]{1,0:T(8,128)(2,1)} async-done(((bf16[128,1536]{1,0:T(8,128)(2,1)}), bf16[128,1536]{1,0:T(8,128)(2,1)}) %all-reduce.10.cloned.1.call-update) | async-done | bytes 393232 | tf_op jit(solution)/shard_map/psum | solution.py:55
  351.3 10.7 %fusion.28 = bf16[128,6144]{1,0:T(8,128)(2,1)} fusion(bf16[1,1536,6144]{2,1,0:T(8,128)(2,1)} %param.8, bf16[128,1536]{1,0:T(8,128)(2,1)} %all-reduce.10.cloned.1.call-done, bf16[1,1,128,1536]{3,2,1,0:T(8,128)(2,1)S(1)} %all-gather.5), kind=kOutput, calls=%fused_computation.26 | convolution fusion | flops 2420834304 | bytes 21233664 | tf_op jit(solution)/shard_map/dot_general | solution.py:60
  362.1 35.5 %reduce-scatter.10.cloned.1.call-done = bf16[128,1536]{1,0:T(8,128)(2,1)} async-done(((bf16[128,6144]{1,0:T(8,128)(2,1)}), bf16[128,1536]{1,0:T(8,128)(2,1)}) %reduce-scatter.10.cloned.1.call-update) | async-done | bytes 393232 | tf_op jit(solution)/shard_map/reduce_scatter | solution.py:61
  397.6 1.2 bitcast_dynamic-update-slice_fusion.1
  398.8 1.3 collective-permute-start.2
  400.1 2.3 collective-permute-done.2
  403.4 39.9 %all-gather.26.cloned.1.call-done = bf16[128,6144]{1,0:T(8,128)(2,1)} async-done(((bf16[128,1536]{1,0:T(8,128)(2,1)}), bf16[128,6144]{1,0:T(8,128)(2,1)}) %all-gather.26.cloned.1.call-update) | async-done | bytes 1572880 | tf_op jit(solution)/shard_map/all_gather | solution.py:49
  443.3 14.0 %fusion.46 = bf16[128,1536]{1,0:T(8,128)(2,1)} fusion(bf16[128,6144]{1,0:T(8,128)(2,1)} %all-gather.26.cloned.1.call-done, bf16[1,1536,6144]{2,1,0:T(8,128)(2,1)} %param.9), kind=kOutput, calls=%fused_computation.32 | convolution fusion | flops 2416115712 | bytes 20840448 | tf_op jit(solution)/shard_map/dot_general | solution.py:52
  457.3 7.8 all-gather.7
  465.2 16.9 %all-reduce.12.cloned.1.call-done = bf16[128,1536]{1,0:T(8,128)(2,1)} async-done(((bf16[128,1536]{1,0:T(8,128)(2,1)}), bf16[128,1536]{1,0:T(8,128)(2,1)}) %all-reduce.12.cloned.1.call-update) | async-done | bytes 393232 | tf_op jit(solution)/shard_map/psum | solution.py:55
  482.1 10.7 %fusion.31 = bf16[128,6144]{1,0:T(8,128)(2,1)} fusion(bf16[1,1536,6144]{2,1,0:T(8,128)(2,1)} %param.8, bf16[128,1536]{1,0:T(8,128)(2,1)} %all-reduce.12.cloned.1.call-done, bf16[1,1,128,1536]{3,2,1,0:T(8,128)(2,1)S(1)} %all-gather.7), kind=kOutput, calls=%fused_computation.27 | convolution fusion | flops 2420834304 | bytes 21233664 | tf_op jit(solution)/shard_map/dot_general | solution.py:60
  493.6 34.8 %reduce-scatter.12.cloned.1.call-done = bf16[128,1536]{1,0:T(8,128)(2,1)} async-done(((bf16[128,6144]{1,0:T(8,128)(2,1)}), bf16[128,1536]{1,0:T(8,128)(2,1)}) %reduce-scatter.12.cloned.1.call-update) | async-done | bytes 393232 | tf_op jit(solution)/shard_map/reduce_scatter | solution.py:61
  528.4 1.4 bitcast_dynamic-update-slice_fusion
  529.8 1.3 collective-permute-start.3
  531.1 2.3 collective-permute-done.3
  533.4 0.8 bitcast_select_fusion.3
  534.3 3.1 constant_dynamic-slice_fusion.3
  539.2 35.2 %all-gather.28.cloned.1.call-done = bf16[128,6144]{1,0:T(8,128)(2,1)} async-done(((bf16[128,1536]{1,0:T(8,128)(2,1)}), bf16[128,6144]{1,0:T(8,128)(2,1)}) %all-gather.28.cloned.1.call-update) | async-done | bytes 1572880 | tf_op jit(solution)/shard_map/all_gather | solution.py:49
  574.3 14.0 %fusion.49 = bf16[128,1536]{1,0:T(8,128)(2,1)} fusion(bf16[128,6144]{1,0:T(8,128)(2,1)} %all-gather.28.cloned.1.call-done, bf16[1,1536,6144]{2,1,0:T(8,128)(2,1)} %param.9), kind=kOutput, calls=%fused_computation.33 | convolution fusion | flops 2416115712 | bytes 20840448 | tf_op jit(solution)/shard_map/dot_general | solution.py:52
  589.2 6.7 all-gather.9
  595.9 14.9 %fusion.61 = f32[1536,6144]{1,0:T(8,128)} fusion(bf16[1,128,6144]{2,1,0:T(8,128)(2,1)S(1)} %copy-done.2, bf16[1,1,128,1536]{3,2,1,0:T(8,128)(2,1)S(1)} %all-gather.1), kind=kOutput, calls=%fused_computation.78 | convolution fusion | flops 2417885184 | bytes 39714816 | tf_op jit(solution)/shard_map/dot_general | solution.py:65
  610.8 0.8 all-gather.32.cloned.1.call-done
  611.7 16.8 %fusion.59 = f32[1536,6144]{1,0:T(8,128)} fusion(bf16[1,1,128,6144]{3,2,1,0:T(8,128)(2,1)} %all-gather.32.cloned.1.call-done, bf16[128,1536]{1,0:T(8,128)(2,1)} %all-reduce.6.cloned.1.call-done, bf16[1,1,128,1536]{3,2,1,0:T(8,128)(2,1)S(1)} %all-gather.1), kind=kOutput, calls=%fused_computation.76 | convolution fusion | flops 2420047872 | bytes 40108032 | tf_op jit(solution)/shard_map/dot_general | solution.py:68
  628.5 14.9 %fusion.121 = f32[1536,6144]{1,0:T(8,128)} fusion(bf16[128,6144]{1,0:T(8,128)(2,1)S(1)} %copy-done.3, bf16[1,1,128,1536]{3,2,1,0:T(8,128)(2,1)S(1)} %copy-done.7), kind=kOutput, calls=%fused_computation.142 | convolution fusion | flops 2417885184 | bytes 39714816 | tf_op jit(solution)/shard_map/dot_general | solution.py:65
  643.4 6.2 all-gather.34.cloned.1.call-done
  649.6 16.7 %fusion.57 = f32[1536,6144]{1,0:T(8,128)} fusion(bf16[1,1,128,6144]{3,2,1,0:T(8,128)(2,1)} %all-gather.34.cloned.1.call-done, bf16[128,1536]{1,0:T(8,128)(2,1)S(1)} %copy-done.20, bf16[1,1,128,1536]{3,2,1,0:T(8,128)(2,1)S(1)} %copy-done.7), kind=kOutput, calls=%fused_computation.74 | convolution fusion | flops 2420047872 | bytes 40108032 | tf_op jit(solution)/shard_map/dot_general | solution.py:68
  666.3 15.4 %fusion.123 = f32[1536,6144]{1,0:T(8,128)} fusion(bf16[128,6144]{1,0:T(8,128)(2,1)S(1)} %copy-done.4, bf16[1,1,128,1536]{3,2,1,0:T(8,128)(2,1)S(1)} %copy-done.9), kind=kOutput, calls=%fused_computation.143 | convolution fusion | flops 2417885184 | bytes 39714816 | tf_op jit(solution)/shard_map/dot_general | solution.py:65
  681.6 5.9 all-gather.36.cloned.1.call-done
  687.5 16.6 %fusion.55 = f32[1536,6144]{1,0:T(8,128)} fusion(bf16[1,1,128,6144]{3,2,1,0:T(8,128)(2,1)} %all-gather.36.cloned.1.call-done, bf16[128,1536]{1,0:T(8,128)(2,1)S(1)} %copy-done.21, bf16[1,1,128,1536]{3,2,1,0:T(8,128)(2,1)S(1)} %copy-done.9), kind=kOutput, calls=%fused_computation.72 | convolution fusion | flops 2420047872 | bytes 40108032 | tf_op jit(solution)/shard_map/dot_general | solution.py:68
  704.1 14.9 %fusion.125 = f32[1536,6144]{1,0:T(8,128)} fusion(bf16[128,6144]{1,0:T(8,128)(2,1)S(1)} %copy-done.5, bf16[1,1,128,1536]{3,2,1,0:T(8,128)(2,1)S(1)} %copy-done.11), kind=kOutput, calls=%fused_computation.144 | convolution fusion | flops 2417885184 | bytes 39714816 | tf_op jit(solution)/shard_map/dot_general | solution.py:65
  719.0 5.9 all-gather.38.cloned.1.call-done
  724.8 16.4 %fusion.53 = f32[1536,6144]{1,0:T(8,128)} fusion(bf16[1,1,128,6144]{3,2,1,0:T(8,128)(2,1)} %all-gather.38.cloned.1.call-done, bf16[128,1536]{1,0:T(8,128)(2,1)S(1)} %copy-done.22, bf16[1,1,128,1536]{3,2,1,0:T(8,128)(2,1)S(1)} %copy-done.11), kind=kOutput, calls=%fused_computation.70 | convolution fusion | flops 2420047872 | bytes 40108032 | tf_op jit(solution)/shard_map/dot_general | solution.py:68
  741.2 0.9 copy.17
  742.1 25.1 %fusion.1 = bf16[1,1536,6144]{2,1,0:T(8,128)(2,1)} fusion(bf16[128,6144]{1,0:T(8,128)(2,1)S(1)} %copy-done.1, f32[1536,6144]{1,0:T(8,128)} %fusion.125, f32[1536,6144]{1,0:T(8,128)} %fusion.123, f32[1536,6144]{1,0:T(8,128)} %fusion.121, f32[1536,6144]{1,0:T(8,128)} %fusion.61, pred[]{:T(512)S(6)} %and.20, pred[]{:T(512)S(6)} %and.19, pred[]{:T(512)S(6)} %and.18, ...), kind=kOutput, calls=%fused_computation.3 | convolution fusion | flops 2512257024 | bytes 171835392 | tf_op jit(solution)/shard_map/dot_general | solution.py:65
  767.3 10.8 %fusion.34 = bf16[128,6144]{1,0:T(8,128)(2,1)} fusion(bf16[1,1536,6144]{2,1,0:T(8,128)(2,1)} %param.8, bf16[128,1536]{1,0:T(8,128)(2,1)} %all-reduce.14.cloned.1.call-done, bf16[1,1,128,1536]{3,2,1,0:T(8,128)(2,1)S(1)} %copy-done.15), kind=kOutput, calls=%fused_computation.28 | convolution fusion | flops 2420834304 | bytes 21233664 | tf_op jit(solution)/shard_map/dot_general | solution.py:60
  778.1 12.7 %all-gather.40.cloned.1.call-done = bf16[1,1,128,6144]{3,2,1,0:T(8,128)(2,1)} async-done(((bf16[1,1,128,1536]{3,2,1,0:T(8,128)(2,1)}), bf16[1,1,128,6144]{3,2,1,0:T(8,128)(2,1)}) %all-gather.40.cloned.1.call-update) | async-done | bytes 1572880 | tf_op jit(solution)/shard_map/all_gather | solution.py:50
  790.9 25.9 %fusion = bf16[1,1536,6144]{2,1,0:T(8,128)(2,1)} fusion(f32[1536,6144]{1,0:T(8,128)} %fusion.53, f32[1536,6144]{1,0:T(8,128)} %fusion.55, f32[1536,6144]{1,0:T(8,128)} %fusion.57, f32[1536,6144]{1,0:T(8,128)} %fusion.59, pred[]{:T(512)S(6)} %and.20, pred[]{:T(512)S(6)} %and.19, pred[]{:T(512)S(6)} %and.18, pred[]{:T(512)S(6)} %and.17, pred[]{:T(512)S(6)} %and.16, ...), kind=kOutput, calls=%fused_computation.2 | convolution fusion | flops 2514419712 | bytes 172228608 | tf_op jit(solution)/shard_map/dot_general | solution.py:68
  816.8 10.6 %reduce-scatter.14.cloned.1.call-done = bf16[128,1536]{1,0:T(8,128)(2,1)} async-done(((bf16[128,6144]{1,0:T(8,128)(2,1)}), bf16[128,1536]{1,0:T(8,128)(2,1)}) %reduce-scatter.14.cloned.1.call-update) | async-done | bytes 393232 | tf_op jit(solution)/shard_map/reduce_scatter | solution.py:61
  827.3 1.1 fusion.130
  828.5 0.9 copy-done.18
  (94 shorter events, 7.0 us)
Async XLA Ops:
  7.2 56.8 %copy-start.16 = (bf16[1,2,64,1536]{3,2,1,0:T(8,128)(2,1)S(1)}, bf16[1,2,64,1536]{3,2,1,0:T(8,128)(2,1)}, u32[]{:S(2)}) copy-start(bf16[1,2,64,1536]{3,2,1,0:T(8,128)(2,1)} %param.7) | copy-start | bytes 1179652
  7.2 42.7 %all-gather.30.cloned.1.call-start = ((), (), s32[]{:S(2)}) async-start(), calls=%async_computation.19 | async-start | bytes 1966080 | tf_op jit(solution)/shard_map/all_gather | solution.py:49
  9.1 80.4 %all-reduce.6.cloned.1.call-start = ((), (), s32[]{:S(2)}) async-start(), calls=%async_computation.5 | async-start | bytes 786432 | tf_op jit(solution)/shard_map/psum | solution.py:55
  63.9 71.9 %copy-start = (bf16[2,128,1536]{2,1,0:T(8,128)(2,1)S(1)}, bf16[2,128,1536]{2,1,0:T(8,128)(2,1)}, u32[]{:S(2)}) copy-start(bf16[2,128,1536]{2,1,0:T(8,128)(2,1)} %param.5) | copy-start | bytes 2359300
  63.9 71.9 %reduce-scatter.6.cloned.1.call-start = ((), (), s32[]{:S(2)}) async-start(), calls=%async_computation.6 | async-start | bytes 1966080 | tf_op jit(solution)/shard_map/reduce_scatter | solution.py:61
  100.2 81.4 %all-gather.22.cloned.1.call-start = ((), (), s32[]{:S(2)}) async-start(), calls=%async_computation.7 | async-start | bytes 1966080 | tf_op jit(solution)/shard_map/all_gather | solution.py:49
  137.0 3.6 collective-permute-start
  141.4 79.0 %all-reduce.8.cloned.1.call-start = ((), (), s32[]{:S(2)}) async-start(), calls=%async_computation.8 | async-start | bytes 786432 | tf_op jit(solution)/shard_map/psum | solution.py:55
  195.5 71.2 %copy-start.12 = (bf16[128,1536]{1,0:T(8,128)(2,1)S(1)}, bf16[128,1536]{1,0:T(8,128)(2,1)}, u32[]{:S(2)}) copy-start(bf16[128,1536]{1,0:T(8,128)(2,1)} %bitcast_select_fusion.6) | copy-start | bytes 1179652
  195.5 71.2 %reduce-scatter.8.cloned.1.call-start = ((), (), s32[]{:S(2)}) async-start(), calls=%async_computation.9 | async-start | bytes 1966080 | tf_op jit(solution)/shard_map/reduce_scatter | solution.py:61
  203.8 122.6 %copy-start.6 = (bf16[1,1,128,1536]{3,2,1,0:T(8,128)(2,1)}, bf16[1,1,128,1536]{3,2,1,0:T(8,128)(2,1)S(1)}, u32[]{:S(2)}) copy-start(bf16[1,1,128,1536]{3,2,1,0:T(8,128)(2,1)S(1)} %all-gather.3) | copy-start | bytes 1179652
  231.1 81.3 %all-gather.24.cloned.1.call-start = ((), (), s32[]{:S(2)}) async-start(), calls=%async_computation.10 | async-start | bytes 1966080 | tf_op jit(solution)/shard_map/all_gather | solution.py:49
  267.9 3.6 collective-permute-start.1
  272.3 79.0 %all-reduce.10.cloned.1.call-start = ((), (), s32[]{:S(2)}) async-start(), calls=%async_computation.11 | async-start | bytes 786432 | tf_op jit(solution)/shard_map/psum | solution.py:55
  326.4 71.2 %copy-start.13 = (bf16[128,1536]{1,0:T(8,128)(2,1)S(1)}, bf16[128,1536]{1,0:T(8,128)(2,1)}, u32[]{:S(2)}) copy-start(bf16[128,1536]{1,0:T(8,128)(2,1)} %bitcast_select_fusion.5) | copy-start | bytes 1179652
  326.4 71.2 %reduce-scatter.10.cloned.1.call-start = ((), (), s32[]{:S(2)}) async-start(), calls=%async_computation.12 | async-start | bytes 1966080 | tf_op jit(solution)/shard_map/reduce_scatter | solution.py:61
  334.7 122.5 %copy-start.8 = (bf16[1,1,128,1536]{3,2,1,0:T(8,128)(2,1)}, bf16[1,1,128,1536]{3,2,1,0:T(8,128)(2,1)S(1)}, u32[]{:S(2)}) copy-start(bf16[1,1,128,1536]{3,2,1,0:T(8,128)(2,1)S(1)} %all-gather.5) | copy-start | bytes 1179652
  362.0 81.3 %all-gather.26.cloned.1.call-start = ((), (), s32[]{:S(2)}) async-start(), calls=%async_computation.13 | async-start | bytes 1966080 | tf_op jit(solution)/shard_map/all_gather | solution.py:49
  398.8 3.6 collective-permute-start.2
  403.2 78.9 %all-reduce.12.cloned.1.call-start = ((), (), s32[]{:S(2)}) async-start(), calls=%async_computation.14 | async-start | bytes 786432 | tf_op jit(solution)/shard_map/psum | solution.py:55
  457.3 71.1 %reduce-scatter.12.cloned.1.call-start = ((), (), s32[]{:S(2)}) async-start(), calls=%async_computation.15 | async-start | bytes 1966080 | tf_op jit(solution)/shard_map/reduce_scatter | solution.py:61
  465.2 16.9 %copy-start.10 = (bf16[1,1,128,1536]{3,2,1,0:T(8,128)(2,1)}, bf16[1,1,128,1536]{3,2,1,0:T(8,128)(2,1)S(1)}, u32[]{:S(2)}) copy-start(bf16[1,1,128,1536]{3,2,1,0:T(8,128)(2,1)S(1)} %all-gather.7) | copy-start | bytes 1179652
  492.7 103.2 %copy-start.2 = (bf16[1,128,6144]{2,1,0:T(8,128)(2,1)S(1)}, bf16[1,128,6144]{2,1,0:T(8,128)(2,1)}, u32[]{:S(2)}) copy-start(bf16[1,128,6144]{2,1,0:T(8,128)(2,1)} %all-gather.30.cloned.1.call-done) | copy-start | bytes 4718596
  492.8 81.5 %all-gather.28.cloned.1.call-start = ((), (), s32[]{:S(2)}) async-start(), calls=%async_computation.16 | async-start | bytes 1966080 | tf_op jit(solution)/shard_map/all_gather | solution.py:49
  529.8 3.6 collective-permute-start.3
  534.2 55.0 %copy-start.19 = (bf16[1,1,64,1536]{3,2,1,0:T(8,128)(2,1)S(1)}, bf16[1,1,64,1536]{3,2,1,0:T(8,128)(2,1)}, u32[]{:S(2)}) copy-start(bf16[1,1,64,1536]{3,2,1,0:T(8,128)(2,1)} %get-tuple-element.16) | copy-start | bytes 589828
  534.2 77.5 %all-gather.32.cloned.1.call-start = ((), (), s32[]{:S(2)}) async-start(), calls=%async_computation.20 | async-start | bytes 1966080 | tf_op jit(solution)/shard_map/all_gather | solution.py:50
  537.4 112.2 %all-gather.34.cloned.1.call-start = ((), (), s32[]{:S(2)}) async-start(), calls=%async_computation.21 | async-start | bytes 1966080 | tf_op jit(solution)/shard_map/all_gather | solution.py:50
  538.0 149.5 %all-gather.36.cloned.1.call-start = ((), (), s32[]{:S(2)}) async-start(), calls=%async_computation.22 | async-start | bytes 1966080 | tf_op jit(solution)/shard_map/all_gather | solution.py:50
  538.5 186.3 %all-gather.38.cloned.1.call-start = ((), (), s32[]{:S(2)}) async-start(), calls=%async_computation.23 | async-start | bytes 1966080 | tf_op jit(solution)/shard_map/all_gather | solution.py:50
  539.1 228.1 %all-reduce.14.cloned.1.call-start = ((), (), s32[]{:S(2)}) async-start(), calls=%async_computation.17 | async-start | bytes 786432 | tf_op jit(solution)/shard_map/psum | solution.py:55
  588.4 202.5 %all-gather.40.cloned.1.call-start = ((), (), s32[]{:S(2)}) async-start(), calls=%async_computation.24 | async-start | bytes 1966080 | tf_op jit(solution)/shard_map/all_gather | solution.py:50
  589.1 238.2 %reduce-scatter.14.cloned.1.call-start = ((), (), s32[]{:S(2)}) async-start(), calls=%async_computation.18 | async-start | bytes 1966080 | tf_op jit(solution)/shard_map/reduce_scatter | solution.py:61
  610.8 17.7 %copy-start.3 = (bf16[128,6144]{1,0:T(8,128)(2,1)S(1)}, bf16[128,6144]{1,0:T(8,128)(2,1)}, u32[]{:S(2)}) copy-start(bf16[128,6144]{1,0:T(8,128)(2,1)} %all-gather.22.cloned.1.call-done) | copy-start | bytes 4718596
  610.8 17.7 %copy-start.7 = (bf16[1,1,128,1536]{3,2,1,0:T(8,128)(2,1)S(1)}, bf16[1,1,128,1536]{3,2,1,0:T(8,128)(2,1)}, u32[]{:S(2)}) copy-start(bf16[1,1,128,1536]{3,2,1,0:T(8,128)(2,1)} %copy-done.6) | copy-start | bytes 1179652
  628.5 21.1 %copy-start.20 = (bf16[128,1536]{1,0:T(8,128)(2,1)S(1)}, bf16[128,1536]{1,0:T(8,128)(2,1)}, u32[]{:S(2)}) copy-start(bf16[128,1536]{1,0:T(8,128)(2,1)} %all-reduce.8.cloned.1.call-done) | copy-start | bytes 1179652
  643.4 22.9 %copy-start.4 = (bf16[128,6144]{1,0:T(8,128)(2,1)S(1)}, bf16[128,6144]{1,0:T(8,128)(2,1)}, u32[]{:S(2)}) copy-start(bf16[128,6144]{1,0:T(8,128)(2,1)} %all-gather.24.cloned.1.call-done) | copy-start | bytes 4718596
  643.4 22.9 %copy-start.9 = (bf16[1,1,128,1536]{3,2,1,0:T(8,128)(2,1)S(1)}, bf16[1,1,128,1536]{3,2,1,0:T(8,128)(2,1)}, u32[]{:S(2)}) copy-start(bf16[1,1,128,1536]{3,2,1,0:T(8,128)(2,1)} %copy-done.8) | copy-start | bytes 1179652
  666.3 21.2 %copy-start.21 = (bf16[128,1536]{1,0:T(8,128)(2,1)S(1)}, bf16[128,1536]{1,0:T(8,128)(2,1)}, u32[]{:S(2)}) copy-start(bf16[128,1536]{1,0:T(8,128)(2,1)} %all-reduce.10.cloned.1.call-done) | copy-start | bytes 1179652
  681.6 22.5 %copy-start.5 = (bf16[128,6144]{1,0:T(8,128)(2,1)S(1)}, bf16[128,6144]{1,0:T(8,128)(2,1)}, u32[]{:S(2)}) copy-start(bf16[128,6144]{1,0:T(8,128)(2,1)} %all-gather.26.cloned.1.call-done) | copy-start | bytes 4718596
  681.6 22.5 %copy-start.11 = (bf16[1,1,128,1536]{3,2,1,0:T(8,128)(2,1)S(1)}, bf16[1,1,128,1536]{3,2,1,0:T(8,128)(2,1)}, u32[]{:S(2)}) copy-start(bf16[1,1,128,1536]{3,2,1,0:T(8,128)(2,1)} %copy-done.10) | copy-start | bytes 1179652
  704.1 20.7 %copy-start.22 = (bf16[128,1536]{1,0:T(8,128)(2,1)S(1)}, bf16[128,1536]{1,0:T(8,128)(2,1)}, u32[]{:S(2)}) copy-start(bf16[128,1536]{1,0:T(8,128)(2,1)} %all-reduce.12.cloned.1.call-done) | copy-start | bytes 1179652
  719.0 23.2 %copy-start.1 = (bf16[128,6144]{1,0:T(8,128)(2,1)S(1)}, bf16[128,6144]{1,0:T(8,128)(2,1)}, u32[]{:S(2)}) copy-start(bf16[128,6144]{1,0:T(8,128)(2,1)} %all-gather.28.cloned.1.call-done) | copy-start | bytes 4718596
  719.0 23.2 %copy-start.15 = (bf16[1,1,128,1536]{3,2,1,0:T(8,128)(2,1)S(1)}, bf16[1,1,128,1536]{3,2,1,0:T(8,128)(2,1)}, u32[]{:S(2)}) copy-start(bf16[1,1,128,1536]{3,2,1,0:T(8,128)(2,1)} %all-gather.9) | copy-start | bytes 1179652
  767.2 23.6 %copy-start.23 = (bf16[128,1536]{1,0:T(8,128)(2,1)S(1)}, bf16[128,1536]{1,0:T(8,128)(2,1)}, u32[]{:S(2)}) copy-start(bf16[128,1536]{1,0:T(8,128)(2,1)} %all-reduce.14.cloned.1.call-done) | copy-start | bytes 1179652
  778.1 49.2 %copy-start.14 = (bf16[128,1536]{1,0:T(8,128)(2,1)S(1)}, bf16[128,1536]{1,0:T(8,128)(2,1)}, u32[]{:S(2)}) copy-start(bf16[128,1536]{1,0:T(8,128)(2,1)} %bitcast_select_fusion.3) | copy-start | bytes 1179652
  778.1 49.2 %copy-start.17 = (bf16[1,2,128,1536]{3,2,1,0:T(8,128)(2,1)S(1)}, bf16[1,2,128,1536]{3,2,1,0:T(8,128)(2,1)}, u32[]{:S(2)}) copy-start(bf16[1,2,128,1536]{3,2,1,0:T(8,128)(2,1)} %copy.17) | copy-start | bytes 2359300
  828.5 0.9 copy-start.18
Sparse Core Ops, SparseCore 0:
  10.1 39.7 all-gather.29
  64.0 25.3 all-reduce.5
  100.3 35.4 reduce-scatter.5
  141.5 39.9 all-gather.21
  195.6 24.7 all-reduce.7
  231.2 35.4 reduce-scatter.7
  272.4 39.9 all-gather.23
  326.5 24.7 all-reduce.9
  362.1 35.4 reduce-scatter.9
  403.3 39.9 all-gather.25
  457.4 24.6 all-reduce.11
  492.9 35.4 reduce-scatter.11
  534.3 39.9 all-gather.27
  575.7 35.8 all-gather.31
  613.6 35.8 all-gather.33
  651.6 35.8 all-gather.35
  688.9 35.8 all-gather.37
  727.0 24.6 all-reduce.13
  753.8 37.0 all-gather.39
  793.0 34.2 reduce-scatter.13
where the time goes:
time: 843 us; the launch traced here: 836 us
  waiting for transfers between devices  456 us (54%)
  matrix products  301 us (36%)
  blocking collectives  40.5 us (5%)
  between operations  14.8 us (2%)
  other arithmetic  9.16 us (1%)
  local copies, waits for them, and re-layouts  8.44 us (1%)
    all_gather x5, waiting for transfers between devices, on_device(): lax.all_gather(current, 'tensor', axis=1, tiled=True)  195 us
    reduce_scatter x5, waiting for transfers between devices, on_device(): lax.psum_scatter(partial_value.astype(jnp.bfloat16), 'tensor', scatter_di...  152 us
    dot_general x5, matrix products, on_device(): lax.dot_general(head_delta, input_cols, contract, preferred_element_type=...  92.4 us
    dot_general x5, matrix products, on_device(): lax.dot_general(activated, grad_cols, contract, preferred_element_type=jn...  85.1 us
    dot_general x5, matrix products, on_device(): lax.dot_general(grad_cols, local_out, (((1,), (1,)), ((), ())), preferred...  69.8 us
    psum x5, waiting for transfers between devices, on_device(): lax.psum(head_part.astype(jnp.bfloat16), 'dp').astype(jnp.float32)  65.3 us
    dot_general x5, matrix products, on_device(): jnp.dot(head_delta, local_in, preferred_element_type=jnp.float32)  53.6 us
    all_gather x5, blocking collectives, on_device(): pre_all = lax.all_gather(pre_local, 'dp', axis=0, tiled=True)  40.5 us
  transfers between devices with their start and end apart: 24, of which 23 were waited for; matrix products, arithmetic and copies ran while one was open for 25% of the time, Pallas kernels for 0%

commit v1 on v0

--- a/solution.py
+++ b/solution.py
@@ -3,6 +3,28 @@
 import jax.numpy as jnp
 from jax import lax
 from jax.sharding import PartitionSpec as P
+from jax.lax import axis_index, axis_size, ppermute
+
+
+def terms_turn(group_axis, tile_in):
+    reached, n_now, tall = (axis_size(group_axis), axis_index(group_axis), tile_in.shape[1])
+    gallery = tuple(((k0, (k0 + 1) % reached) for k0 in range(reached)))
+    store = tuple(((k0, (k0 - 1) % reached) for k0 in range(reached)))
+    g_now = jnp.zeros((*tile_in.shape[:1], reached * tall, *tile_in.shape[2:]), tile_in.dtype)
+    g_now = lax.dynamic_update_slice_in_dim(g_now, tile_in, n_now * tall, axis=1)
+    z_new = response = tile_in
+    a_next = reached // 2
+    ii = 1
+    while ii < a_next + 1:
+        z_new = ppermute(z_new, axis_name=group_axis, perm=gallery)
+        g_now = lax.dynamic_update_slice_in_dim(g_now, z_new, (n_now - ii) % reached * tall, axis=1)
+        if ii < reached - a_next:
+            response = ppermute(response, perm=store, axis_name=group_axis)
+            g_now = lax.dynamic_update_slice_in_dim(
+                g_now, response, (n_now + ii) % reached * tall, axis=1
+            )
+        ii = ii + 1
+    return g_now
 
 
 def shifted(block, axis, distance):
@@ -46,7 +68,7 @@
         layer_input = lax.dynamic_index_in_dim(inputs[0], clipped, 0, False)
         pre_local = lax.dynamic_index_in_dim(pre[0], clipped, 0, False)
         grad_cols, input_cols = (
-            lax.all_gather(current, "tensor", axis=1, tiled=True),
+            terms_turn("tensor", tile_in=current),
             lax.all_gather(layer_input, "tensor", axis=1, tiled=True),
         )
         head_part = lax.dot_general(

time: 843 us -> 794 us (0.942)
  waiting for transfers between devices: 456 us -> 375 us
  starting transfers between devices: 6.98 us -> 36.3 us
    all_gather x5 -> x0, waiting for transfers between devices: 195 us -> none  [on_device(): lax.all_gather(current, 'tensor', axis=1, tiled=True)]
    ppermute x0 -> x15, waiting for transfers between devices: none -> 133 us  [the longest x10 90.2 us: terms_turn(): z_new = ppermute(z_new, axis_name=group_axis, perm=gallery)]
    all_gather x5, waiting for transfers between devices: 31.5 us -> 0.03 us  [on_device(): lax.all_gather(layer_input, 'tensor', axis=1, tiled=True)]
    ppermute x0 -> x15, starting transfers between devices: none -> 30.5 us  [the longest x5 16.8 us: terms_turn(): response = ppermute(response, perm=store, axis_name=group_axis)]
    psum x5, waiting for transfers between devices: 65.3 us -> 80.3 us  [on_device(): lax.psum(head_part.astype(jnp.bfloat16), 'dp').astype(jnp.float32)]
  transfers between devices with their start and end apart: 24 -> 34, of which waited for: 23 -> 28; matrix products, arithmetic and copies ran while one was open for 25% -> 27% of each run, Pallas kernels for 0% -> 0%
where the time goes in v1:
time: 794 us; the launch traced here: 784 us
  waiting for transfers between devices  375 us (47%)
  matrix products  302 us (38%)
  blocking collectives  37 us (5%)
  starting transfers between devices  36.3 us (5%)
  between operations  14.8 us (2%)
  local copies, waits for them, and re-layouts  9.64 us (1%)
  other arithmetic  9.35 us (1%)
    reduce_scatter x5, waiting for transfers between devices, on_device(): lax.psum_scatter(partial_value.astype(jnp.bfloat16), 'tensor', scatter_di...  150 us
    dot_general x5, matrix products, on_device(): lax.dot_general(head_delta, input_cols, contract, preferred_element_type=...  93.1 us
    ppermute x10, waiting for transfers between devices, terms_turn(): z_new = ppermute(z_new, axis_name=group_axis, perm=gallery)  90.2 us
    dot_general x5, matrix products, on_device(): lax.dot_general(activated, grad_cols, contract, preferred_element_type=jn...  86.2 us
    psum x5, waiting for transfers between devices, on_device(): lax.psum(head_part.astype(jnp.bfloat16), 'dp').astype(jnp.float32)  80.3 us
    dot_general x5, matrix products, on_device(): lax.dot_general(grad_cols, local_out, (((1,), (1,)), ((), ())), preferred...  68.9 us
    dot_general x5, matrix products, on_device(): jnp.dot(head_delta, local_in, preferred_element_type=jnp.float32)  53.4 us
    ppermute x5, waiting for transfers between devices, terms_turn(): response = ppermute(response, perm=store, axis_name=group_axis)  42.7 us
  transfers between devices with their start and end apart: 34, of which 28 were waited for; matrix products, arithmetic and copies ran while one was open for 27% of the time, Pallas kernels for 0%

profile of v1, /device:TPU:0, one launch (start us, length us, event | category | flops | bytes accessed | tf_op | source)
XLA Modules:
  0.0 784.1 jit_solution(11475580243056568774)
XLA Ops:
  8.4 3.1 collective-permute-start
  11.5 2.1 collective-permute-start.1
  13.6 9.9 %collective-permute-done = bf16[128,1536]{1,0:T(8,128)(2,1)S(1)} collective-permute-done((bf16[128,1536]{1,0:T(8,128)(2,1)S(1)}, bf16[128,1536]{1,0:T(8,128)(2,1)S(1)}, u32[]{:S(2)}, u32[]{:S(2)}) %collective-permute-start) | collective-permute-done | bytes 393248 | tf_op jit(solution)/shard_map/ppermute | solution.py:19
  23.6 7.1 collective-permute-done.1
  30.8 8.8 %collective-permute-done.2 = bf16[128,1536]{1,0:T(8,128)(2,1)S(1)} collective-permute-done((bf16[128,1536]{1,0:T(8,128)(2,1)S(1)}, bf16[128,1536]{1,0:T(8,128)(2,1)S(1)}, u32[]{:S(2)}, u32[]{:S(2)}) %collective-permute-start.2) | collective-permute-done | bytes 393248 | tf_op jit(solution)/shard_map/ppermute | solution.py:19
  39.6 14.0 %fusion.37 = bf16[128,1536]{1,0:T(8,128)(2,1)} fusion(bf16[128,6144]{1,0:T(8,128)(2,1)S(1)} %constant_dynamic-update-slice_fusion.16, bf16[1,1536,6144]{2,1,0:T(8,128)(2,1)} %param.9), kind=kOutput, calls=%fused_computation.29 | convolution fusion | flops 2416115712 | bytes 20840448 | tf_op jit(solution)/shard_map/dot_general | solution.py:74
  54.6 8.7 %all-gather = bf16[1,1,128,1536]{3,2,1,0:T(8,128)(2,1)S(1)} all-gather(bf16[1,1,64,1536]{3,2,1,0:T(8,128)(2,1)S(1)} %get-tuple-element.29), channel_id=2, replica_groups=mesh['pipe'=4,'dp'=2,'tensor'=4] {'dp'}, dimensions={2}, use_global_device_ids=true | all-gather | bytes 589824 | tf_op jit(solution)/shard_map/all_gather | solution.py:78
  63.3 15.6 %all-reduce.6.cloned.1.call-done = bf16[128,1536]{1,0:T(8,128)(2,1)} async-done(((bf16[128,1536]{1,0:T(8,128)(2,1)}), bf16[128,1536]{1,0:T(8,128)(2,1)}) %all-reduce.6.cloned.1.call-update) | async-done | bytes 393232 | tf_op jit(solution)/shard_map/psum | solution.py:77
  78.9 10.7 %fusion.22 = bf16[128,6144]{1,0:T(8,128)(2,1)} fusion(bf16[1,1536,6144]{2,1,0:T(8,128)(2,1)} %param.8, bf16[128,1536]{1,0:T(8,128)(2,1)} %all-reduce.6.cloned.1.call-done, bf16[1,1,128,1536]{3,2,1,0:T(8,128)(2,1)S(1)} %all-gather), kind=kOutput, calls=%fused_computation.24 | convolution fusion | flops 2420834304 | bytes 21233664 | tf_op jit(solution)/shard_map/dot_general | solution.py:82
  89.7 35.5 %reduce-scatter.6.cloned.1.call-done = bf16[128,1536]{1,0:T(8,128)(2,1)} async-done(((bf16[128,6144]{1,0:T(8,128)(2,1)}), bf16[128,1536]{1,0:T(8,128)(2,1)}) %reduce-scatter.6.cloned.1.call-update) | async-done | bytes 393232 | tf_op jit(solution)/shard_map/reduce_scatter | solution.py:83
  126.5 1.3 collective-permute-start.3
  127.8 2.4 collective-permute-done.3
  131.7 3.7 collective-permute-start.5
  135.4 5.9 collective-permute-done.4
  141.6 9.8 %collective-permute-done.5 = bf16[128,1536]{1,0:T(8,128)(2,1)S(1)} collective-permute-done((bf16[128,1536]{1,0:T(8,128)(2,1)S(1)}, bf16[128,1536]{1,0:T(8,128)(2,1)S(1)}, u32[]{:S(2)}, u32[]{:S(2)}) %collective-permute-start.5) | collective-permute-done | bytes 393248 | tf_op jit(solution)/shard_map/ppermute | solution.py:22
  151.4 6.4 collective-permute-done.6
  157.8 13.5 %fusion.40 = bf16[128,1536]{1,0:T(8,128)(2,1)} fusion(bf16[128,6144]{1,0:T(8,128)(2,1)S(1)} %constant_dynamic-update-slice_fusion.12, bf16[1,1536,6144]{2,1,0:T(8,128)(2,1)} %param.9), kind=kOutput, calls=%fused_computation.30 | convolution fusion | flops 2416115712 | bytes 20840448 | tf_op jit(solution)/shard_map/dot_general | solution.py:74
  171.4 6.3 all-gather.2
  177.7 21.9 %all-reduce.8.cloned.1.call-done = bf16[128,1536]{1,0:T(8,128)(2,1)} async-done(((bf16[128,1536]{1,0:T(8,128)(2,1)}), bf16[128,1536]{1,0:T(8,128)(2,1)}) %all-reduce.8.cloned.1.call-update) | async-done | bytes 393232 | tf_op jit(solution)/shard_map/psum | solution.py:77
  199.6 10.7 %fusion.25 = bf16[128,6144]{1,0:T(8,128)(2,1)} fusion(bf16[1,1536,6144]{2,1,0:T(8,128)(2,1)} %param.8, bf16[128,1536]{1,0:T(8,128)(2,1)} %all-reduce.8.cloned.1.call-done, bf16[1,1,128,1536]{3,2,1,0:T(8,128)(2,1)S(1)} %all-gather.2), kind=kOutput, calls=%fused_computation.25 | convolution fusion | flops 2420834304 | bytes 21233664 | tf_op jit(solution)/shard_map/dot_general | solution.py:82
  210.4 35.5 %reduce-scatter.8.cloned.1.call-done = bf16[128,1536]{1,0:T(8,128)(2,1)} async-done(((bf16[128,6144]{1,0:T(8,128)(2,1)}), bf16[128,1536]{1,0:T(8,128)(2,1)}) %reduce-scatter.8.cloned.1.call-update) | async-done | bytes 393232 | tf_op jit(solution)/shard_map/reduce_scatter | solution.py:83
  247.2 1.3 collective-permute-start.7
  248.5 2.3 collective-permute-done.7
  251.3 3.7 collective-permute-start.9
  255.0 5.9 collective-permute-done.8
  261.4 9.7 %collective-permute-done.9 = bf16[128,1536]{1,0:T(8,128)(2,1)S(1)} collective-permute-done((bf16[128,1536]{1,0:T(8,128)(2,1)S(1)}, bf16[128,1536]{1,0:T(8,128)(2,1)S(1)}, u32[]{:S(2)}, u32[]{:S(2)}) %collective-permute-start.9) | collective-permute-done | bytes 393248 | tf_op jit(solution)/shard_map/ppermute | solution.py:22
  271.1 6.1 collective-permute-done.10
  277.3 14.0 %fusion.43 = bf16[128,1536]{1,0:T(8,128)(2,1)} fusion(bf16[128,6144]{1,0:T(8,128)(2,1)S(1)} %constant_dynamic-update-slice_fusion.8, bf16[1,1536,6144]{2,1,0:T(8,128)(2,1)} %param.9), kind=kOutput, calls=%fused_computation.31 | convolution fusion | flops 2416115712 | bytes 20840448 | tf_op jit(solution)/shard_map/dot_general | solution.py:74
  291.3 6.5 all-gather.4
  297.9 21.4 %all-reduce.10.cloned.1.call-done = bf16[128,1536]{1,0:T(8,128)(2,1)} async-done(((bf16[128,1536]{1,0:T(8,128)(2,1)}), bf16[128,1536]{1,0:T(8,128)(2,1)}) %all-reduce.10.cloned.1.call-update) | async-done | bytes 393232 | tf_op jit(solution)/shard_map/psum | solution.py:77
  319.3 10.7 %fusion.28 = bf16[128,6144]{1,0:T(8,128)(2,1)} fusion(bf16[1,1536,6144]{2,1,0:T(8,128)(2,1)} %param.8, bf16[128,1536]{1,0:T(8,128)(2,1)} %all-reduce.10.cloned.1.call-done, bf16[1,1,128,1536]{3,2,1,0:T(8,128)(2,1)S(1)} %all-gather.4), kind=kOutput, calls=%fused_computation.26 | convolution fusion | flops 2420834304 | bytes 21233664 | tf_op jit(solution)/shard_map/dot_general | solution.py:82
  331.1 34.5 %reduce-scatter.10.cloned.1.call-done = bf16[128,1536]{1,0:T(8,128)(2,1)} async-done(((bf16[128,6144]{1,0:T(8,128)(2,1)}), bf16[128,1536]{1,0:T(8,128)(2,1)}) %reduce-scatter.10.cloned.1.call-update) | async-done | bytes 393232 | tf_op jit(solution)/shard_map/reduce_scatter | solution.py:83
  366.9 1.3 collective-permute-start.11
  368.2 2.3 collective-permute-done.11
  371.0 3.7 collective-permute-start.13
  374.7 5.9 collective-permute-done.12
  380.7 10.0 %collective-permute-done.13 = bf16[128,1536]{1,0:T(8,128)(2,1)S(1)} collective-permute-done((bf16[128,1536]{1,0:T(8,128)(2,1)S(1)}, bf16[128,1536]{1,0:T(8,128)(2,1)S(1)}, u32[]{:S(2)}, u32[]{:S(2)}) %collective-permute-start.13) | collective-permute-done | bytes 393248 | tf_op jit(solution)/shard_map/ppermute | solution.py:22
  390.8 6.1 collective-permute-done.14
  397.0 14.0 %fusion.46 = bf16[128,1536]{1,0:T(8,128)(2,1)} fusion(bf16[128,6144]{1,0:T(8,128)(2,1)S(1)} %constant_dynamic-update-slice_fusion.4, bf16[1,1536,6144]{2,1,0:T(8,128)(2,1)} %param.9), kind=kOutput, calls=%fused_computation.32 | convolution fusion | flops 2416115712 | bytes 20840448 | tf_op jit(solution)/shard_map/dot_general | solution.py:74
  411.1 6.5 all-gather.6
  417.6 21.5 %all-reduce.12.cloned.1.call-done = bf16[128,1536]{1,0:T(8,128)(2,1)} async-done(((bf16[128,1536]{1,0:T(8,128)(2,1)}), bf16[128,1536]{1,0:T(8,128)(2,1)}) %all-reduce.12.cloned.1.call-update) | async-done | bytes 393232 | tf_op jit(solution)/shard_map/psum | solution.py:77
  439.1 10.7 %fusion.31 = bf16[128,6144]{1,0:T(8,128)(2,1)} fusion(bf16[1,1536,6144]{2,1,0:T(8,128)(2,1)} %param.8, bf16[128,1536]{1,0:T(8,128)(2,1)} %all-reduce.12.cloned.1.call-done, bf16[1,1,128,1536]{3,2,1,0:T(8,128)(2,1)S(1)} %all-gather.6), kind=kOutput, calls=%fused_computation.27 | convolution fusion | flops 2420834304 | bytes 21233664 | tf_op jit(solution)/shard_map/dot_general | solution.py:82
  453.7 31.7 %reduce-scatter.12.cloned.1.call-done = bf16[128,1536]{1,0:T(8,128)(2,1)} async-done(((bf16[128,6144]{1,0:T(8,128)(2,1)}), bf16[128,1536]{1,0:T(8,128)(2,1)}) %reduce-scatter.12.cloned.1.call-update) | async-done | bytes 393232 | tf_op jit(solution)/shard_map/reduce_scatter | solution.py:83
  485.4 1.9 bitcast_dynamic-update-slice_fusion
  488.7 2.6 collective-permute-done.15
  492.9 3.7 collective-permute-start.17
  496.6 16.6 %collective-permute-done.16 = bf16[128,1536]{1,0:T(8,128)(2,1)S(1)} collective-permute-done((bf16[128,1536]{1,0:T(8,128)(2,1)S(1)}, bf16[128,1536]{1,0:T(8,128)(2,1)S(1)}, u32[]{:S(2)}, u32[]{:S(2)}) %collective-permute-start.16) | collective-permute-done | bytes 393248 | tf_op jit(solution)/shard_map/ppermute | solution.py:19
  513.2 8.9 %collective-permute-start.18 = (bf16[128,1536]{1,0:T(8,128)(2,1)S(1)}, bf16[128,1536]{1,0:T(8,128)(2,1)S(1)}, u32[]{:S(2)}, u32[]{:S(2)}) collective-permute-start(bf16[128,1536]{1,0:T(8,128)(2,1)S(1)} %collective-permute-done.16), channel_id=1, source_target_pairs={{0,1},{1,2},{2,3},{3,0},{4,5},{5,6},{6,7},{7,4},{8,9},{9,10},{10,1... | collective-permute-start | bytes 1179656 | tf_op jit(solution)/shard_map/ppermute | solution.py:19
  522.1 6.0 collective-permute-done.17
  528.2 18.7 %collective-permute-done.18 = bf16[128,1536]{1,0:T(8,128)(2,1)S(1)} collective-permute-done((bf16[128,1536]{1,0:T(8,128)(2,1)S(1)}, bf16[128,1536]{1,0:T(8,128)(2,1)S(1)}, u32[]{:S(2)}, u32[]{:S(2)}) %collective-permute-start.18) | collective-permute-done | bytes 393248 | tf_op jit(solution)/shard_map/ppermute | solution.py:19
  546.9 13.5 %fusion.49 = bf16[128,1536]{1,0:T(8,128)(2,1)} fusion(bf16[128,6144]{1,0:T(8,128)(2,1)S(1)} %constant_dynamic-update-slice_fusion, bf16[1,1536,6144]{2,1,0:T(8,128)(2,1)} %param.9), kind=kOutput, calls=%fused_computation.33 | convolution fusion | flops 2416115712 | bytes 20840448 | tf_op jit(solution)/shard_map/dot_general | solution.py:74
  561.1 8.9 %all-gather.8 = bf16[1,1,128,1536]{3,2,1,0:T(8,128)(2,1)} all-gather(bf16[1,1,64,1536]{3,2,1,0:T(8,128)(2,1)} %get-tuple-element.26), channel_id=10, replica_groups=mesh['pipe'=4,'dp'=2,'tensor'=4] {'dp'}, dimensions={2}, use_global_device_ids=true | all-gather | bytes 589824 | tf_op jit(solution)/shard_map/all_gather | solution.py:78
  570.0 16.1 %fusion.116 = f32[1536,6144]{1,0:T(8,128)} fusion(bf16[128,6144]{1,0:T(8,128)(2,1)} %copy-done.4, bf16[1,1,128,1536]{3,2,1,0:T(8,128)(2,1)S(1)} %all-gather), kind=kOutput, calls=%fused_computation.138 | convolution fusion | flops 2417885184 | bytes 39714816 | tf_op jit(solution)/shard_map/dot_general | solution.py:87
  586.1 16.7 %fusion.59 = f32[1536,6144]{1,0:T(8,128)} fusion(bf16[1,1,128,6144]{3,2,1,0:T(8,128)(2,1)} %all-gather.16.cloned.1.call-done, bf16[128,1536]{1,0:T(8,128)(2,1)} %all-reduce.6.cloned.1.call-done, bf16[1,1,128,1536]{3,2,1,0:T(8,128)(2,1)S(1)} %all-gather), kind=kOutput, calls=%fused_computation.76 | convolution fusion | flops 2420047872 | bytes 40108032 | tf_op jit(solution)/shard_map/dot_general | solution.py:90
  602.8 14.9 %fusion.118 = f32[1536,6144]{1,0:T(8,128)} fusion(bf16[128,6144]{1,0:T(8,128)(2,1)S(1)} %constant_dynamic-update-slice_fusion.12, bf16[1,1,128,1536]{3,2,1,0:T(8,128)(2,1)S(1)} %copy-done.17), kind=kOutput, calls=%fused_computation.139 | convolution fusion | flops 2417885184 | bytes 39714816 | tf_op jit(solution)/shard_map/dot_general | solution.py:87
  617.7 17.0 %fusion.57 = f32[1536,6144]{1,0:T(8,128)} fusion(bf16[1,1,128,6144]{3,2,1,0:T(8,128)(2,1)} %all-gather.18.cloned.1.call-done, bf16[128,1536]{1,0:T(8,128)(2,1)} %all-reduce.8.cloned.1.call-done, bf16[1,1,128,1536]{3,2,1,0:T(8,128)(2,1)S(1)} %copy-done.18), kind=kOutput, calls=%fused_computation.74 | convolution fusion | flops 2420047872 | bytes 40108032 | tf_op jit(solution)/shard_map/dot_general | solution.py:90
  634.7 15.3 %fusion.120 = f32[1536,6144]{1,0:T(8,128)} fusion(bf16[128,6144]{1,0:T(8,128)(2,1)S(1)} %copy-done.1, bf16[1,1,128,1536]{3,2,1,0:T(8,128)(2,1)S(1)} %copy-done.20), kind=kOutput, calls=%fused_computation.140 | convolution fusion | flops 2417885184 | bytes 39714816 | tf_op jit(solution)/shard_map/dot_general | solution.py:87
  650.0 16.7 %fusion.55 = f32[1536,6144]{1,0:T(8,128)} fusion(bf16[1,1,128,6144]{3,2,1,0:T(8,128)(2,1)} %all-gather.20.cloned.1.call-done, bf16[128,1536]{1,0:T(8,128)(2,1)} %all-reduce.10.cloned.1.call-done, bf16[1,1,128,1536]{3,2,1,0:T(8,128)(2,1)S(1)} %copy-done.21), kind=kOutput, calls=%fused_computation.72 | convolution fusion | flops 2420047872 | bytes 40108032 | tf_op jit(solution)/shard_map/dot_general | solution.py:90
  666.7 15.0 %fusion.122 = f32[1536,6144]{1,0:T(8,128)} fusion(bf16[128,6144]{1,0:T(8,128)(2,1)S(1)} %copy-done.3, bf16[1,1,128,1536]{3,2,1,0:T(8,128)(2,1)S(1)} %copy-done.23), kind=kOutput, calls=%fused_computation.141 | convolution fusion | flops 2417885184 | bytes 39714816 | tf_op jit(solution)/shard_map/dot_general | solution.py:87
  681.7 17.0 %fusion.53 = f32[1536,6144]{1,0:T(8,128)} fusion(bf16[1,1,128,6144]{3,2,1,0:T(8,128)(2,1)} %all-gather.22.cloned.1.call-done, bf16[128,1536]{1,0:T(8,128)(2,1)} %all-reduce.12.cloned.1.call-done, bf16[1,1,128,1536]{3,2,1,0:T(8,128)(2,1)S(1)} %copy-done.24), kind=kOutput, calls=%fused_computation.70 | convolution fusion | flops 2420047872 | bytes 40108032 | tf_op jit(solution)/shard_map/dot_general | solution.py:90
  699.6 24.9 %fusion.1 = bf16[1,1536,6144]{2,1,0:T(8,128)(2,1)} fusion(bf16[128,6144]{1,0:T(8,128)(2,1)S(1)} %constant_dynamic-update-slice_fusion, f32[1536,6144]{1,0:T(8,128)} %fusion.122, f32[1536,6144]{1,0:T(8,128)} %fusion.120, f32[1536,6144]{1,0:T(8,128)} %fusion.118, f32[1536,6144]{1,0:T(8,128)} %fusion.116, pred[]{:T(512)S(6)} %and.49, pred[]{:T(512)S(6)} %and.48, ...), kind=kOutput, calls=%fused_computation.3 | convolution fusion | flops 2512257024 | bytes 171835392 | tf_op jit(solution)/shard_map/dot_general | solution.py:87
  724.6 10.7 %fusion.34 = bf16[128,6144]{1,0:T(8,128)(2,1)} fusion(bf16[1,1536,6144]{2,1,0:T(8,128)(2,1)} %param.8, bf16[128,1536]{1,0:T(8,128)(2,1)} %all-reduce.14.cloned.1.call-done, bf16[1,1,128,1536]{3,2,1,0:T(8,128)(2,1)S(1)} %copy-done.25), kind=kOutput, calls=%fused_computation.28 | convolution fusion | flops 2420834304 | bytes 21233664 | tf_op jit(solution)/shard_map/dot_general | solution.py:82
  736.3 25.8 %fusion = bf16[1,1536,6144]{2,1,0:T(8,128)(2,1)} fusion(f32[1536,6144]{1,0:T(8,128)} %fusion.53, f32[1536,6144]{1,0:T(8,128)} %fusion.55, f32[1536,6144]{1,0:T(8,128)} %fusion.57, f32[1536,6144]{1,0:T(8,128)} %fusion.59, pred[]{:T(512)S(6)} %and.49, pred[]{:T(512)S(6)} %and.48, pred[]{:T(512)S(6)} %and.47, pred[]{:T(512)S(6)} %and.46, pred[]{:T(512)S(6)} %and.42, ...), kind=kOutput, calls=%fused_computation.2 | convolution fusion | flops 2514419712 | bytes 172228608 | tf_op jit(solution)/shard_map/dot_general | solution.py:90
  762.1 13.2 %reduce-scatter.14.cloned.1.call-done = bf16[128,1536]{1,0:T(8,128)(2,1)} async-done(((bf16[128,6144]{1,0:T(8,128)(2,1)}), bf16[128,1536]{1,0:T(8,128)(2,1)}) %reduce-scatter.14.cloned.1.call-update) | async-done | bytes 393232 | tf_op jit(solution)/shard_map/reduce_scatter | solution.py:83
  (157 shorter events, 22.7 us)
Async XLA Ops:
  7.2 71.7 %all-reduce.6.cloned.1.call-start = ((), (), s32[]{:S(2)}) async-start(), calls=%async_computation.5 | async-start | bytes 786432 | tf_op jit(solution)/shard_map/psum | solution.py:77
  8.4 15.1 %collective-permute-start = (bf16[128,1536]{1,0:T(8,128)(2,1)S(1)}, bf16[128,1536]{1,0:T(8,128)(2,1)S(1)}, u32[]{:S(2)}, u32[]{:S(2)}) collective-permute-start(bf16[128,1536]{1,0:T(8,128)(2,1)S(1)} %get-tuple-element.20), channel_id=1, source_target_pairs={{0,1},{1,2},{2,3},{3,0},{4,5},{5,6},{6,7},{7,4},{8,9},{9,10},{10,1... | collective-permute-start | bytes 1179656 | tf_op jit(solution)/shard_map/ppermute | solution.py:19
  11.5 19.2 %collective-permute-start.1 = (bf16[128,1536]{1,0:T(8,128)(2,1)S(1)}, bf16[128,1536]{1,0:T(8,128)(2,1)S(1)}, u32[]{:S(2)}, u32[]{:S(2)}) collective-permute-start(bf16[128,1536]{1,0:T(8,128)(2,1)S(1)} %get-tuple-element.20), channel_id=1, source_target_pairs={{0,3},{1,0},{2,1},{3,2},{4,7},{5,4},{6,5},{7,6},{8,11},{9,8},{10,9... | collective-permute-start | bytes 1179656 | tf_op jit(solution)/shard_map/ppermute | solution.py:22
  23.5 16.0 %collective-permute-start.2 = (bf16[128,1536]{1,0:T(8,128)(2,1)S(1)}, bf16[128,1536]{1,0:T(8,128)(2,1)S(1)}, u32[]{:S(2)}, u32[]{:S(2)}) collective-permute-start(bf16[128,1536]{1,0:T(8,128)(2,1)S(1)} %collective-permute-done), channel_id=1, source_target_pairs={{0,1},{1,2},{2,3},{3,0},{4,5},{5,6},{6,7},{7,4},{8,9},{9,10},{10,1... | collective-permute-start | bytes 1179656 | tf_op jit(solution)/shard_map/ppermute | solution.py:19
  39.6 14.0 %copy-start.4 = (bf16[128,6144]{1,0:T(8,128)(2,1)}, bf16[128,6144]{1,0:T(8,128)(2,1)S(1)}, u32[]{:S(2)}) copy-start(bf16[128,6144]{1,0:T(8,128)(2,1)S(1)} %constant_dynamic-update-slice_fusion.16) | copy-start | bytes 4718596
  39.6 14.1 %copy-start.26 = (bf16[1,2,64,1536]{3,2,1,0:T(8,128)(2,1)S(1)}, bf16[1,2,64,1536]{3,2,1,0:T(8,128)(2,1)}, u32[]{:S(2)}) copy-start(bf16[1,2,64,1536]{3,2,1,0:T(8,128)(2,1)} %param.7) | copy-start | bytes 1179652
  53.6 71.6 %reduce-scatter.6.cloned.1.call-start = ((), (), s32[]{:S(2)}) async-start(), calls=%async_computation.6 | async-start | bytes 1966080 | tf_op jit(solution)/shard_map/reduce_scatter | solution.py:83
  89.6 110.0 %all-reduce.8.cloned.1.call-start = ((), (), s32[]{:S(2)}) async-start(), calls=%async_computation.7 | async-start | bytes 786432 | tf_op jit(solution)/shard_map/psum | solution.py:77
  125.2 5.1 copy-start.12
  126.5 3.7 collective-permute-start.3
  131.5 19.9 %copy-start.29 = (bf16[128,1536]{1,0:T(8,128)(2,1)}, bf16[128,1536]{1,0:T(8,128)(2,1)S(1)}, u32[]{:S(2)}) copy-start(bf16[128,1536]{1,0:T(8,128)(2,1)S(1)} %get-tuple-element.18) | copy-start | bytes 1179652
  131.5 9.7 %collective-permute-start.4 = (bf16[128,1536]{1,0:T(8,128)(2,1)S(1)}, bf16[128,1536]{1,0:T(8,128)(2,1)S(1)}, u32[]{:S(2)}, u32[]{:S(2)}) collective-permute-start(bf16[128,1536]{1,0:T(8,128)(2,1)S(1)} %get-tuple-element.18), channel_id=1, source_target_pairs={{0,1},{1,2},{2,3},{3,0},{4,5},{5,6},{6,7},{7,4},{8,9},{9,10},{10,1... | collective-permute-start | bytes 1179656 | tf_op jit(solution)/shard_map/ppermute | solution.py:19
  131.7 19.6 %collective-permute-start.5 = (bf16[128,1536]{1,0:T(8,128)(2,1)S(1)}, bf16[128,1536]{1,0:T(8,128)(2,1)S(1)}, u32[]{:S(2)}, u32[]{:S(2)}) collective-permute-start(bf16[128,1536]{1,0:T(8,128)(2,1)S(1)} %get-tuple-element.18), channel_id=1, source_target_pairs={{0,3},{1,0},{2,1},{3,2},{4,7},{5,4},{6,5},{7,6},{8,11},{9,8},{10,9... | collective-permute-start | bytes 1179656 | tf_op jit(solution)/shard_map/ppermute | solution.py:22
  141.3 16.5 %collective-permute-start.6 = (bf16[128,1536]{1,0:T(8,128)(2,1)S(1)}, bf16[128,1536]{1,0:T(8,128)(2,1)S(1)}, u32[]{:S(2)}, u32[]{:S(2)}) collective-permute-start(bf16[128,1536]{1,0:T(8,128)(2,1)S(1)} %collective-permute-done.4), channel_id=1, source_target_pairs={{0,1},{1,2},{2,3},{3,0},{4,5},{5,6},{6,7},{7,4},{8,9},{9,10},{10,1... | collective-permute-start | bytes 1179656 | tf_op jit(solution)/shard_map/ppermute | solution.py:19
  157.8 13.6 %copy-start.36 = (bf16[1,1,64,1536]{3,2,1,0:T(8,128)(2,1)S(1)}, bf16[1,1,64,1536]{3,2,1,0:T(8,128)(2,1)}, u32[]{:S(2)}) copy-start(bf16[1,1,64,1536]{3,2,1,0:T(8,128)(2,1)} %get-tuple-element.28) | copy-start | bytes 589828
  171.3 74.6 %reduce-scatter.8.cloned.1.call-start = ((), (), s32[]{:S(2)}) async-start(), calls=%async_computation.8 | async-start | bytes 1966080 | tf_op jit(solution)/shard_map/reduce_scatter | solution.py:83
  177.7 32.6 %copy-start.16 = (bf16[1,1,128,1536]{3,2,1,0:T(8,128)(2,1)}, bf16[1,1,128,1536]{3,2,1,0:T(8,128)(2,1)S(1)}, u32[]{:S(2)}) copy-start(bf16[1,1,128,1536]{3,2,1,0:T(8,128)(2,1)S(1)} %all-gather.2) | copy-start | bytes 1179652
  210.3 35.6 %copy-start.30 = (bf16[128,1536]{1,0:T(8,128)(2,1)S(1)}, bf16[128,1536]{1,0:T(8,128)(2,1)}, u32[]{:S(2)}) copy-start(bf16[128,1536]{1,0:T(8,128)(2,1)} %copy-done.29) | copy-start | bytes 1179652
  210.3 109.0 %all-reduce.10.cloned.1.call-start = ((), (), s32[]{:S(2)}) async-start(), calls=%async_computation.9 | async-start | bytes 786432 | tf_op jit(solution)/shard_map/psum | solution.py:77
  245.9 5.0 copy-start.13
  247.2 3.6 collective-permute-start.7
  251.1 20.1 %copy-start.31 = (bf16[128,1536]{1,0:T(8,128)(2,1)}, bf16[128,1536]{1,0:T(8,128)(2,1)S(1)}, u32[]{:S(2)}) copy-start(bf16[128,1536]{1,0:T(8,128)(2,1)S(1)} %get-tuple-element.16) | copy-start | bytes 1179652
  251.1 9.7 %collective-permute-start.8 = (bf16[128,1536]{1,0:T(8,128)(2,1)S(1)}, bf16[128,1536]{1,0:T(8,128)(2,1)S(1)}, u32[]{:S(2)}, u32[]{:S(2)}) collective-permute-start(bf16[128,1536]{1,0:T(8,128)(2,1)S(1)} %get-tuple-element.16), channel_id=1, source_target_pairs={{0,1},{1,2},{2,3},{3,0},{4,5},{5,6},{6,7},{7,4},{8,9},{9,10},{10,1... | collective-permute-start | bytes 1179656 | tf_op jit(solution)/shard_map/ppermute | solution.py:19
  251.3 19.8 %collective-permute-start.9 = (bf16[128,1536]{1,0:T(8,128)(2,1)S(1)}, bf16[128,1536]{1,0:T(8,128)(2,1)S(1)}, u32[]{:S(2)}, u32[]{:S(2)}) collective-permute-start(bf16[128,1536]{1,0:T(8,128)(2,1)S(1)} %get-tuple-element.16), channel_id=1, source_target_pairs={{0,3},{1,0},{2,1},{3,2},{4,7},{5,4},{6,5},{7,6},{8,11},{9,8},{10,9... | collective-permute-start | bytes 1179656 | tf_op jit(solution)/shard_map/ppermute | solution.py:22
  260.8 16.4 %collective-permute-start.10 = (bf16[128,1536]{1,0:T(8,128)(2,1)S(1)}, bf16[128,1536]{1,0:T(8,128)(2,1)S(1)}, u32[]{:S(2)}, u32[]{:S(2)}) collective-permute-start(bf16[128,1536]{1,0:T(8,128)(2,1)S(1)} %collective-permute-done.8), channel_id=1, source_target_pairs={{0,1},{1,2},{2,3},{3,0},{4,5},{5,6},{6,7},{7,4},{8,9},{9,10},{10,1... | collective-permute-start | bytes 1179656 | tf_op jit(solution)/shard_map/ppermute | solution.py:19
  277.3 14.0 %copy-start = (bf16[128,6144]{1,0:T(8,128)(2,1)}, bf16[128,6144]{1,0:T(8,128)(2,1)S(1)}, u32[]{:S(2)}) copy-start(bf16[128,6144]{1,0:T(8,128)(2,1)S(1)} %constant_dynamic-update-slice_fusion.8) | copy-start | bytes 4718596
  291.3 74.3 %reduce-scatter.10.cloned.1.call-start = ((), (), s32[]{:S(2)}) async-start(), calls=%async_computation.10 | async-start | bytes 1966080 | tf_op jit(solution)/shard_map/reduce_scatter | solution.py:83
  297.9 21.4 %copy-start.19 = (bf16[1,1,128,1536]{3,2,1,0:T(8,128)(2,1)}, bf16[1,1,128,1536]{3,2,1,0:T(8,128)(2,1)S(1)}, u32[]{:S(2)}) copy-start(bf16[1,1,128,1536]{3,2,1,0:T(8,128)(2,1)S(1)} %all-gather.4) | copy-start | bytes 1179652
  330.0 35.6 %copy-start.32 = (bf16[128,1536]{1,0:T(8,128)(2,1)S(1)}, bf16[128,1536]{1,0:T(8,128)(2,1)}, u32[]{:S(2)}) copy-start(bf16[128,1536]{1,0:T(8,128)(2,1)} %copy-done.31) | copy-start | bytes 1179652
  330.0 109.1 %all-reduce.12.cloned.1.call-start = ((), (), s32[]{:S(2)}) async-start(), calls=%async_computation.11 | async-start | bytes 786432 | tf_op jit(solution)/shard_map/psum | solution.py:77
  365.6 5.0 copy-start.14
  366.9 3.6 collective-permute-start.11
  370.8 20.0 %copy-start.27 = (bf16[128,1536]{1,0:T(8,128)(2,1)}, bf16[128,1536]{1,0:T(8,128)(2,1)S(1)}, u32[]{:S(2)}) copy-start(bf16[128,1536]{1,0:T(8,128)(2,1)S(1)} %get-tuple-element.14) | copy-start | bytes 1179652
  370.8 9.7 %collective-permute-start.12 = (bf16[128,1536]{1,0:T(8,128)(2,1)S(1)}, bf16[128,1536]{1,0:T(8,128)(2,1)S(1)}, u32[]{:S(2)}, u32[]{:S(2)}) collective-permute-start(bf16[128,1536]{1,0:T(8,128)(2,1)S(1)} %get-tuple-element.14), channel_id=1, source_target_pairs={{0,1},{1,2},{2,3},{3,0},{4,5},{5,6},{6,7},{7,4},{8,9},{9,10},{10,1... | collective-permute-start | bytes 1179656 | tf_op jit(solution)/shard_map/ppermute | solution.py:19
  371.0 19.8 %collective-permute-start.13 = (bf16[128,1536]{1,0:T(8,128)(2,1)S(1)}, bf16[128,1536]{1,0:T(8,128)(2,1)S(1)}, u32[]{:S(2)}, u32[]{:S(2)}) collective-permute-start(bf16[128,1536]{1,0:T(8,128)(2,1)S(1)} %get-tuple-element.14), channel_id=1, source_target_pairs={{0,3},{1,0},{2,1},{3,2},{4,7},{5,4},{6,5},{7,6},{8,11},{9,8},{10,9... | collective-permute-start | bytes 1179656 | tf_op jit(solution)/shard_map/ppermute | solution.py:22
  380.5 16.4 %collective-permute-start.14 = (bf16[128,1536]{1,0:T(8,128)(2,1)S(1)}, bf16[128,1536]{1,0:T(8,128)(2,1)S(1)}, u32[]{:S(2)}, u32[]{:S(2)}) collective-permute-start(bf16[128,1536]{1,0:T(8,128)(2,1)S(1)} %collective-permute-done.12), channel_id=1, source_target_pairs={{0,1},{1,2},{2,3},{3,0},{4,5},{5,6},{6,7},{7,4},{8,9},{9,10},{10,1... | collective-permute-start | bytes 1179656 | tf_op jit(solution)/shard_map/ppermute | solution.py:19
  397.0 14.0 %copy-start.2 = (bf16[128,6144]{1,0:T(8,128)(2,1)}, bf16[128,6144]{1,0:T(8,128)(2,1)S(1)}, u32[]{:S(2)}) copy-start(bf16[128,6144]{1,0:T(8,128)(2,1)S(1)} %constant_dynamic-update-slice_fusion.4) | copy-start | bytes 4718596
  411.0 74.4 %reduce-scatter.12.cloned.1.call-start = ((), (), s32[]{:S(2)}) async-start(), calls=%async_computation.12 | async-start | bytes 1966080 | tf_op jit(solution)/shard_map/reduce_scatter | solution.py:83
  417.6 32.2 %copy-start.22 = (bf16[1,1,128,1536]{3,2,1,0:T(8,128)(2,1)}, bf16[1,1,128,1536]{3,2,1,0:T(8,128)(2,1)S(1)}, u32[]{:S(2)}) copy-start(bf16[1,1,128,1536]{3,2,1,0:T(8,128)(2,1)S(1)} %all-gather.6) | copy-start | bytes 1179652
  449.8 3.8 copy-start.8
  449.8 136.3 %all-gather.16.cloned.1.call-start = ((), (), s32[]{:S(2)}) async-start(), calls=%async_computation.15 | async-start | bytes 1966080 | tf_op jit(solution)/shard_map/all_gather | solution.py:72
  452.2 33.2 %copy-start.28 = (bf16[128,1536]{1,0:T(8,128)(2,1)S(1)}, bf16[128,1536]{1,0:T(8,128)(2,1)}, u32[]{:S(2)}) copy-start(bf16[128,1536]{1,0:T(8,128)(2,1)} %copy-done.27) | copy-start | bytes 1179652
  452.2 165.4 %all-gather.18.cloned.1.call-start = ((), (), s32[]{:S(2)}) async-start(), calls=%async_computation.16 | async-start | bytes 1966080 | tf_op jit(solution)/shard_map/all_gather | solution.py:72
  452.8 197.1 %all-gather.20.cloned.1.call-start = ((), (), s32[]{:S(2)}) async-start(), calls=%async_computation.17 | async-start | bytes 1966080 | tf_op jit(solution)/shard_map/all_gather | solution.py:72
  453.6 228.1 %all-gather.22.cloned.1.call-start = ((), (), s32[]{:S(2)}) async-start(), calls=%async_computation.18 | async-start | bytes 1966080 | tf_op jit(solution)/shard_map/all_gather | solution.py:72
  487.3 1.4 copy-start.9
  487.3 3.9 collective-permute-start.15
  488.6 236.0 %all-reduce.14.cloned.1.call-start = ((), (), s32[]{:S(2)}) async-start(), calls=%async_computation.13 | async-start | bytes 786432 | tf_op jit(solution)/shard_map/psum | solution.py:77
  492.7 35.5 %copy-start.33 = (bf16[128,1536]{1,0:T(8,128)(2,1)}, bf16[128,1536]{1,0:T(8,128)(2,1)S(1)}, u32[]{:S(2)}) copy-start(bf16[128,1536]{1,0:T(8,128)(2,1)S(1)} %get-tuple-element.12) | copy-start | bytes 1179652
  492.7 20.5 %collective-permute-start.16 = (bf16[128,1536]{1,0:T(8,128)(2,1)S(1)}, bf16[128,1536]{1,0:T(8,128)(2,1)S(1)}, u32[]{:S(2)}, u32[]{:S(2)}) collective-permute-start(bf16[128,1536]{1,0:T(8,128)(2,1)S(1)} %get-tuple-element.12), channel_id=1, source_target_pairs={{0,1},{1,2},{2,3},{3,0},{4,5},{5,6},{6,7},{7,4},{8,9},{9,10},{10,1... | collective-permute-start | bytes 1179656 | tf_op jit(solution)/shard_map/ppermute | solution.py:19
  492.9 35.3 %collective-permute-start.17 = (bf16[128,1536]{1,0:T(8,128)(2,1)S(1)}, bf16[128,1536]{1,0:T(8,128)(2,1)S(1)}, u32[]{:S(2)}, u32[]{:S(2)}) collective-permute-start(bf16[128,1536]{1,0:T(8,128)(2,1)S(1)} %get-tuple-element.12), channel_id=1, source_target_pairs={{0,3},{1,0},{2,1},{3,2},{4,7},{5,4},{6,5},{7,6},{8,11},{9,8},{10,9... | collective-permute-start | bytes 1179656 | tf_op jit(solution)/shard_map/ppermute | solution.py:22
  513.2 33.7 %collective-permute-start.18 = (bf16[128,1536]{1,0:T(8,128)(2,1)S(1)}, bf16[128,1536]{1,0:T(8,128)(2,1)S(1)}, u32[]{:S(2)}, u32[]{:S(2)}) collective-permute-start(bf16[128,1536]{1,0:T(8,128)(2,1)S(1)} %collective-permute-done.16), channel_id=1, source_target_pairs={{0,1},{1,2},{2,3},{3,0},{4,5},{5,6},{6,7},{7,4},{8,9},{9,10},{10,1... | collective-permute-start | bytes 1179656 | tf_op jit(solution)/shard_map/ppermute | solution.py:19
  560.4 174.9 %all-gather.24.cloned.1.call-start = ((), (), s32[]{:S(2)}) async-start(), calls=%async_computation.19 | async-start | bytes 1966080 | tf_op jit(solution)/shard_map/all_gather | solution.py:72
  561.0 214.3 %reduce-scatter.14.cloned.1.call-start = ((), (), s32[]{:S(2)}) async-start(), calls=%async_computation.14 | async-start | bytes 1966080 | tf_op jit(solution)/shard_map/reduce_scatter | solution.py:83
  586.1 16.7 %copy-start.17 = (bf16[1,1,128,1536]{3,2,1,0:T(8,128)(2,1)S(1)}, bf16[1,1,128,1536]{3,2,1,0:T(8,128)(2,1)}, u32[]{:S(2)}) copy-start(bf16[1,1,128,1536]{3,2,1,0:T(8,128)(2,1)} %copy-done.16) | copy-start | bytes 1179652
  602.8 14.9 %copy-start.18 = (bf16[1,1,128,1536]{3,2,1,0:T(8,128)(2,1)S(1)}, bf16[1,1,128,1536]{3,2,1,0:T(8,128)(2,1)}, u32[]{:S(2)}) copy-start(bf16[1,1,128,1536]{3,2,1,0:T(8,128)(2,1)} %copy-done.16) | copy-start | bytes 1179652
  617.7 17.0 %copy-start.1 = (bf16[128,6144]{1,0:T(8,128)(2,1)S(1)}, bf16[128,6144]{1,0:T(8,128)(2,1)}, u32[]{:S(2)}) copy-start(bf16[128,6144]{1,0:T(8,128)(2,1)} %copy-done) | copy-start | bytes 4718596
  617.7 17.0 %copy-start.20 = (bf16[1,1,128,1536]{3,2,1,0:T(8,128)(2,1)S(1)}, bf16[1,1,128,1536]{3,2,1,0:T(8,128)(2,1)}, u32[]{:S(2)}) copy-start(bf16[1,1,128,1536]{3,2,1,0:T(8,128)(2,1)} %copy-done.19) | copy-start | bytes 1179652
  634.7 15.3 %copy-start.21 = (bf16[1,1,128,1536]{3,2,1,0:T(8,128)(2,1)S(1)}, bf16[1,1,128,1536]{3,2,1,0:T(8,128)(2,1)}, u32[]{:S(2)}) copy-start(bf16[1,1,128,1536]{3,2,1,0:T(8,128)(2,1)} %copy-done.19) | copy-start | bytes 1179652
  650.0 16.7 %copy-start.3 = (bf16[128,6144]{1,0:T(8,128)(2,1)S(1)}, bf16[128,6144]{1,0:T(8,128)(2,1)}, u32[]{:S(2)}) copy-start(bf16[128,6144]{1,0:T(8,128)(2,1)} %copy-done.2) | copy-start | bytes 4718596
  650.0 16.7 %copy-start.23 = (bf16[1,1,128,1536]{3,2,1,0:T(8,128)(2,1)S(1)}, bf16[1,1,128,1536]{3,2,1,0:T(8,128)(2,1)}, u32[]{:S(2)}) copy-start(bf16[1,1,128,1536]{3,2,1,0:T(8,128)(2,1)} %copy-done.22) | copy-start | bytes 1179652
  666.7 15.0 %copy-start.24 = (bf16[1,1,128,1536]{3,2,1,0:T(8,128)(2,1)S(1)}, bf16[1,1,128,1536]{3,2,1,0:T(8,128)(2,1)}, u32[]{:S(2)}) copy-start(bf16[1,1,128,1536]{3,2,1,0:T(8,128)(2,1)} %copy-done.22) | copy-start | bytes 1179652
  681.7 17.0 %copy-start.10 = (bf16[2,128,1536]{2,1,0:T(8,128)(2,1)S(1)}, bf16[2,128,1536]{2,1,0:T(8,128)(2,1)}, u32[]{:S(2)}) copy-start(bf16[2,128,1536]{2,1,0:T(8,128)(2,1)} %copy-done.9) | copy-start | bytes 2359300
  735.3 40.0 %copy-start.34 = (bf16[128,1536]{1,0:T(8,128)(2,1)S(1)}, bf16[128,1536]{1,0:T(8,128)(2,1)}, u32[]{:S(2)}) copy-start(bf16[128,1536]{1,0:T(8,128)(2,1)} %copy-done.33) | copy-start | bytes 1179652
  (8 other events, 8.9 us)
Sparse Core Ops, SparseCore 0:
  53.7 25.0 all-reduce.5
  89.7 35.4 reduce-scatter.5
  171.5 28.1 all-reduce.7
  210.4 35.4 reduce-scatter.7
  291.4 27.8 all-reduce.9
  330.1 35.4 reduce-scatter.9
  411.1 27.9 all-reduce.11
  449.9 35.4 reduce-scatter.11
  487.0 58.9 all-gather.15
  547.3 36.1 all-gather.17
  585.1 35.8 all-gather.19
  622.5 35.8 all-gather.21
  660.7 24.6 all-reduce.13
  686.8 37.0 all-gather.23
  735.4 39.8 reduce-scatter.13
